TPU v7x, 32 devices: a whole 2x2x4 slice. The times are simulated.
32 devices in a mesh: px: 4 (over y, x), py: 8 (over z, core).
Axes of the slice: x: 2, y: 2, z: 4, core: 2. Of those that a mesh axis runs over, the one named last changes fastest.
Arguments:
- field: bfloat16 [32, 128, 128, 128], P(None, 'px', 'py'), may hold values from -6 to 6
- spec_fine: bfloat16 [2, 32, 32, 32, 32, 32], P(None, None, None, None, 'px', 'py'), may hold values from -18 to 18
- mix_fine: bfloat16 [32, 32], replicated, may hold values from -1 to 1
- bias_fine: float32 [32], replicated, may hold values from -3 to 3
- spec_coarse: bfloat16 [2, 32, 32, 32, 32, 32], P(None, None, None, None, 'px', 'py'), may hold values from -12 to 12
- mix_coarse: bfloat16 [32, 32], replicated, may hold values from -1 to 1
- bias_coarse: float32 [32], replicated, may hold values from -3 to 3
Outputs:
- output: bfloat16 [32, 128, 128, 128], P(None, 'px', 'py')
All inputs are finite; a program needn't handle non-finite values.
Results may differ from a plain program's by a relative error of at most 0.0085.
Values may be sent and summed in bfloat16 or wider, within the bound.
A program may use at most 192 MiB of HBM per device.

v0:
```python
import functools
import math

import jax
import jax.numpy as jnp
from jax import lax
from jax.experimental import pallas as pl
from jax.experimental.pallas import tpu as pltpu
from jax.sharding import PartitionSpec as P

narrow = jnp.bfloat16
wide = jnp.float32


def phases(cells, modes, offset):
    places = jnp.arange(cells, dtype=jnp.int32)
    frequency = jnp.arange(modes, dtype=jnp.int32) - offset
    windings = places[:, None] * frequency[None, :] % cells
    return windings.astype(wide) * (2.0 * math.pi / cells)


def turn_table(cells, modes, offset, sign):
    angle = phases(cells, modes, offset)
    cos = jnp.cos(angle).astype(narrow)
    sin = (sign * jnp.sin(angle)).astype(narrow)
    return jnp.stack([jnp.stack([cos, sin], -1), jnp.stack([-sin, cos], -1)])


def depth_forward(cells, modes):
    angle = phases(cells, modes, 0)
    return jnp.stack([jnp.cos(angle), -jnp.sin(angle)], 1).astype(narrow)


def depth_inverse(cells, modes):
    angle = phases(cells, modes, 0)
    factor = jnp.where(jnp.arange(modes) == 0, 1.0, 2.0).astype(wide) / float(cells * cells * cells)
    return jnp.stack([factor * jnp.cos(angle), -factor * jnp.sin(angle)]).astype(narrow)


def dot(form, left, right, kind=narrow):
    return jnp.einsum(form, left, right, preferred_element_type=wide).astype(kind)


def swap(value, axis):
    return lax.all_to_all(value, axis, split_axis=0, concat_axis=0)


def mix_modes(modes, spectral):
    mr = modes[:, 0][:, None]
    mi = modes[:, 1][:, None]
    wr = spectral[0].astype(wide)
    wi = spectral[1].astype(wide)
    real = (mr * wr - mi * wi).sum(0)
    imag = (mr * wi + mi * wr).sum(0)
    return jnp.stack([real, imag], 1)


def spectral_coefficients(field, spectral):
    np_, ng = lax.axis_size("px"), lax.axis_size("py")
    c, xl, yl, cells = field.shape
    _, _, _, kx, ml, kl = spectral.shape
    ky, kz = ml * np_, kl * ng
    cb = c // np_
    row = turn_table(cells, kx, kx // 2, -1.0).reshape(2, np_, xl, kx, 2)
    column = turn_table(cells, ky, ky // 2, -1.0).reshape(2, ng, yl, np_, ml, 2)
    depth = depth_forward(cells, kz)
    row_back = turn_table(cells, kx, kx // 2, 1.0).reshape(2, np_, xl, kx, 2)
    column_back = turn_table(cells, ky, ky // 2, 1.0).reshape(2, ng, yl, np_, ml, 2)
    depth_back = depth_inverse(cells, kz)

    d = depth_lines(field.reshape(c, xl * yl, cells), depth.reshape(cells, 2 * kz).T)
    d = swap(d.reshape(np_, cb, 2 * kz, xl * yl), "px").reshape(np_, cb, 2, ng, kl, xl, yl)
    e = dot("pcrgkxy,rpxjs->gcskjy", d, row)
    e = swap(e, "py")
    f = dot("hcskjy,shyqmt->qctjmk", e, column)
    f = swap(f, "px").reshape(c, 2, kx, ml, kl)
    mixed = mix_modes(f.astype(wide), spectral).astype(narrow)
    b = swap(mixed.reshape(np_, cb, 2, kx, ml, kl), "px")
    b = dot("pcujmk,uhypmv->hcvkjy", b, column_back)
    b = swap(b, "py")
    b = dot("gcvkjy,vpxjw->pcwgkxy", b, row_back)
    b = swap(b.reshape(np_, cb, 2 * kz, xl * yl), "px").reshape(c, 2 * kz, xl * yl)
    return b, jnp.transpose(depth_back, (0, 2, 1)).reshape(2 * kz, cells)


def line_tables(shape, split, cell_at, cells, offset, sign):
    near, far, quota = split
    iota = lambda axis: lax.broadcasted_iota(jnp.int32, shape, axis)
    row, column = iota(2), iota(3)
    cell, mode = (row % near, column % far) if cell_at == 0 else (column % far, row % near)
    blocks, part = (iota(0), iota(1)) if cell_at == 0 else (iota(1), iota(0))
    side = near if cell_at == 0 else far
    other = column // (quota * far)
    angle = ((blocks * side + cell) * (mode - offset) % cells).astype(wide) * (2.0 * math.pi / cells)
    sin = jnp.where(other == 1, sign, -sign) * jnp.sin(angle)
    value = jnp.where(part == other, jnp.cos(angle), sin)
    same = row // near == column // far % quota
    return jnp.where(same, value, 0.0).astype(narrow)


def rows_kernel(d, table, out):
    blocks, cs, both, _ = d.shape
    kz = both // 2
    groups, _, _, kl, _ = out.shape
    take, give = table.shape[2], table.shape[3] // 2
    for t in range(d.shape[3] // take):
        total = 0.0
        for p in range(blocks):
            for r in range(2):
                part = d[p, :, r * kz : (r + 1) * kz, t * take : (t + 1) * take]
                part = part.reshape(cs * kz, take)
                total = total + jnp.dot(part, table[p, r], preferred_element_type=wide)
        for s in range(2):
            for c in range(cs):
                for g in range(groups):
                    rows = total[c * kz + g * kl : c * kz + (g + 1) * kl, s * give : (s + 1) * give]
                    out[g, c, s, :, t * give : (t + 1) * give] = rows.astype(narrow)


def rows_call(d, table, groups):
    blocks, cb, both, points = d.shape
    take, give = table.shape[2], table.shape[3] // 2
    width = points // take * give
    kl = both // 2 // groups
    cs = 4 if cb % 4 == 0 else 1
    return pl.pallas_call(
        rows_kernel,
        out_shape=jax.ShapeDtypeStruct((groups, cb, 2, kl, width), narrow),
        grid=(cb // cs,),
        in_specs=[
            pl.BlockSpec((blocks, cs, both, points), lambda i: (0, i, 0, 0)),
            pl.BlockSpec(table.shape, lambda i: (0, 0, 0, 0)),
        ],
        out_specs=pl.BlockSpec((groups, cs, 2, kl, width), lambda i: (0, i, 0, 0, 0)),
        name="rows_call",
    )(d, table)


def rows_back_kernel(b, table, out, lines):
    groups, cs, _, kl, width = b.shape
    blocks = out.shape[0]
    kz = groups * kl
    take, give = table.shape[2], table.shape[3] // 2
    for v in range(2):
        for c in range(cs):
            for g in range(groups):
                at = c * kz + g * kl
                lines[v, at : at + kl, :] = b[g, c, v].astype(wide)
    for t in range(width // take):
        parts = [lines[v, :, t * take : (t + 1) * take].astype(narrow) for v in range(2)]
        for p in range(blocks):
            total = jnp.dot(parts[0], table[0, p], preferred_element_type=wide)
            total = total + jnp.dot(parts[1], table[1, p], preferred_element_type=wide)
            for w in range(2):
                rows = total[:, w * give : (w + 1) * give].reshape(cs, kz, give)
                out[p, :, w * kz : (w + 1) * kz, t * give : (t + 1) * give] = rows.astype(narrow)


def rows_back_call(b, table):
    groups, cb, _, kl, width = b.shape
    blocks = table.shape[1]
    take, give = table.shape[2], table.shape[3] // 2
    points = width // take * give
    kz = groups * kl
    cs = 4 if cb % 4 == 0 else 1
    return pl.pallas_call(
        rows_back_kernel,
        out_shape=jax.ShapeDtypeStruct((blocks, cb, 2 * kz, points), narrow),
        grid=(cb // cs,),
        in_specs=[
            pl.BlockSpec((groups, cs, 2, kl, width), lambda i: (0, i, 0, 0, 0)),
            pl.BlockSpec(table.shape, lambda i: (0, 0, 0, 0)),
        ],
        out_specs=pl.BlockSpec((blocks, cs, 2 * kz, points), lambda i: (0, i, 0, 0)),
        scratch_shapes=[pltpu.VMEM((2, cs * kz, width), wide)],
        name="rows_back_call",
    )(b, table)


def tiled_coefficients(field, spectral):
    np_, ng = lax.axis_size("px"), lax.axis_size("py")
    c, xl, yl, cells = field.shape
    _, _, _, kx, ml, kl = spectral.shape
    ky, kz = ml * np_, kl * ng
    cb = c // np_
    quota = min(yl, 128 // xl)
    row = line_tables(
        (np_, 2, quota * xl, 2 * quota * kx), (xl, kx, quota), 0, cells, kx // 2, -1.0
    )
    column = turn_table(cells, ky, ky // 2, -1.0).reshape(2, ng, yl, np_, ml, 2)
    depth = depth_forward(cells, kz)
    row_back = line_tables(
        (2, np_, quota * kx, 2 * quota * xl), (kx, xl, quota), 1, cells, kx // 2, 1.0
    )
    column_back = turn_table(cells, ky, ky // 2, 1.0).reshape(2, ng, yl, np_, ml, 2)
    depth_back = depth_inverse(cells, kz)

    d = depth_lines(field.reshape(c, xl * yl, cells), depth.reshape(cells, 2 * kz).T, yl)
    d = swap(d.reshape(np_, cb, 2 * kz, xl * yl), "px")
    e = swap(rows_call(d, row, ng), "py")
    e = e.reshape(ng, cb, 2, kl, yl, kx)
    f = dot("hcskyj,shyqmt->qctmkj", e, column)
    f = swap(f, "px").reshape(c, 2, ml, kl, kx)
    mixed = mix_modes(jnp.transpose(f, (0, 1, 4, 2, 3)).astype(wide), spectral).astype(narrow)
    mixed = jnp.transpose(mixed, (0, 1, 3, 4, 2))
    b = swap(mixed.reshape(np_, cb, 2, ml, kl, kx), "px")
    b = dot("pcumkj,uhypmv->hcvkyj", b, column_back)
    b = swap(b.reshape(ng, cb, 2, kl, yl * kx), "py")
    b = swap(rows_back_call(b, row_back), "px")
    b = b.reshape(c, 2 * kz, xl * yl)
    return b, jnp.transpose(depth_back, (0, 2, 1)).reshape(2 * kz, cells)


def gelu(v):
    return 0.5 * v * (1.0 + jnp.tanh(math.sqrt(2.0 / math.pi) * (v + 0.044715 * v * v * v)))


def depth_kernel(yl, table, lines, out, held):
    points = lines.shape[1]
    for i in range(lines.shape[0]):
        cells = lines[i]
        if yl:
            held[...] = cells.astype(wide)
            cells = [held[pl.ds(y, points // yl, yl), :] for y in range(yl)]
            cells = jnp.concatenate(cells, 0).astype(narrow)
        out[i] = lax.dot_general(
            table[...], cells, (((1,), (1,)), ((), ())), preferred_element_type=wide
        ).astype(narrow)


def depth_lines(lines, table, yl=0):
    c, points, cells = lines.shape
    step = 4 if c % 4 == 0 else 1
    return pl.pallas_call(
        functools.partial(depth_kernel, yl),
        out_shape=jax.ShapeDtypeStruct((c, table.shape[0], points), narrow),
        grid=(c // step,),
        in_specs=[
            pl.BlockSpec(table.shape, lambda i: (0, 0)),
            pl.BlockSpec((step, points, cells), lambda i: (i, 0, 0)),
        ],
        out_specs=pl.BlockSpec((step, table.shape[0], points), lambda i: (i, 0, 0)),
        scratch_shapes=[pltpu.VMEM((points, cells), wide)],
        name="depth_lines",
    )(table, lines)


def spread(mixing, rows):
    c = mixing.shape[0]
    place = jnp.arange(c * rows)
    pick = (place[:, None] // rows == jnp.arange(c)[None, :]).astype(narrow)
    full = dot("on,np->op", pick, dot("nc,pc->np", mixing.T, pick), wide)
    return jnp.where(place[:, None] % rows == place[None, :] % rows, full, 0.0).astype(narrow)


def column_of(offsets, rows):
    return jnp.broadcast_to(offsets[:, None], (offsets.shape[0], rows)).reshape(-1, 1)


def back_along_depth(coefficients, table, sums, xl, yl):
    for o in range(sums.shape[0]):
        part = lax.dot_general(
            coefficients[o], table[...], (((0,), (0,)), ((), ())), preferred_element_type=wide
        )
        for y in range(yl):
            sums[o, pl.ds(y, xl, yl), :] = part[y * xl : (y + 1) * xl]


def upper_kernel(field, coefficients, table, mixing, offsets, pairs, upper, pooled, sums, half):
    c, xs, yl, cells = field.shape
    step = pl.program_id(0)

    @pl.when(step == 0)
    def _():
        back_along_depth(coefficients, table, sums, sums.shape[1] // yl, yl)

    for x in range(xs):
        lines = field[:, x].reshape(c * yl, cells)
        total = jnp.dot(mixing[...], lines, preferred_element_type=wide)
        total = total + sums[:, pl.ds(pl.multiple_of((step * xs + x) * yl, 8), yl), :].reshape(c * yl, cells) + offsets[...]
        value = gelu(total).astype(narrow)
        upper[:, x] = value.reshape(c, yl, cells)
        part = jnp.dot(value, pairs[...], preferred_element_type=wide)
        if x % 2 == 0:
            half[...] = part
        else:
            half[...] = half[...] + part
            rows = c * yl // 2
            mean = half[pl.ds(0, rows, 2), :] + half[pl.ds(1, rows, 2), :]
            mean = (mean * 0.125)[:, : cells // 2]
            pooled[:, x // 2] = mean.reshape(c, yl // 2, cells // 2).astype(narrow)


def upper_call(field, coefficients, table, mixing, offsets):
    c, xl, yl, cells = field.shape
    xs = 4
    place = jnp.arange(cells)
    pairs = (place[:, None] // 2 == place[None, :]).astype(narrow)
    whole = lambda value: pl.BlockSpec(value.shape, lambda i: (0,) * value.ndim)
    mixing = spread(mixing, yl)
    offsets = column_of(offsets, yl)
    return pl.pallas_call(
        upper_kernel,
        out_shape=(
            jax.ShapeDtypeStruct(field.shape, narrow),
            jax.ShapeDtypeStruct((c, xl // 2, yl // 2, cells // 2), narrow),
        ),
        grid=(xl // xs,),
        in_specs=[
            pl.BlockSpec((c, xs, yl, cells), lambda i: (0, i, 0, 0)),
            whole(coefficients),
            whole(table),
            whole(mixing),
            whole(offsets),
            whole(pairs),
        ],
        out_specs=(
            pl.BlockSpec((c, xs, yl, cells), lambda i: (0, i, 0, 0)),
            pl.BlockSpec((c, xs // 2, yl // 2, cells // 2), lambda i: (0, i, 0, 0)),
        ),
        scratch_shapes=[
            pltpu.VMEM((c, xl * yl, cells), wide),
            pltpu.VMEM((c * yl, cells), wide),
        ],
        compiler_params=pltpu.CompilerParams(vmem_limit_bytes=48 * 2**20),
        name="upper_call",
    )(field, coefficients, table, mixing, offsets, pairs)


def merge_kernel(upper, pooled, coefficients, table, mixing, offsets, twice, out, sums, lifted):
    c, xs, yl, cells = pooled.shape
    step = pl.program_id(0)

    @pl.when(step == 0)
    def _():
        back_along_depth(coefficients, table, sums, sums.shape[1] // yl, yl)

    for x in range(xs):
        lines = pooled[:, x].astype(wide).reshape(c * yl, cells).astype(narrow)
        total = jnp.dot(mixing[...], lines, preferred_element_type=wide)
        total = total + sums[:, pl.ds(pl.multiple_of((step * xs + x) * yl, 8), yl), :].reshape(c * yl, cells) + offsets[...]
        value = gelu(total).astype(narrow)
        wider = jnp.dot(value, twice[...], preferred_element_type=wide)
        lifted[pl.ds(0, c * yl, 2), :] = wider
        lifted[pl.ds(1, c * yl, 2), :] = wider
        for side in range(2):
            fine = upper[:, 2 * x + side].astype(wide).reshape(2 * c * yl, 2 * cells)
            out[:, 2 * x + side] = (fine + lifted[...]).astype(narrow).reshape(c, 2 * yl, 2 * cells)


def merge_call(upper, pooled, coefficients, table, mixing, offsets):
    c, xl, yl, cells = pooled.shape
    xs = 2
    twice = (jnp.arange(cells)[:, None] == jnp.arange(2 * cells)[None, :] // 2).astype(narrow)
    whole = lambda value: pl.BlockSpec(value.shape, lambda i: (0,) * value.ndim)
    mixing = spread(mixing, yl)
    offsets = column_of(offsets, yl)
    fine = pl.BlockSpec((c, 2 * xs, 2 * yl, 2 * cells), lambda i: (0, i, 0, 0))
    return pl.pallas_call(
        merge_kernel,
        out_shape=jax.ShapeDtypeStruct(upper.shape, narrow),
        grid=(xl // xs,),
        in_specs=[
            fine,
            pl.BlockSpec((c, xs, yl, cells), lambda i: (0, i, 0, 0)),
            whole(coefficients),
            whole(table),
            whole(mixing),
            whole(offsets),
            whole(twice),
        ],
        out_specs=fine,
        scratch_shapes=[
            pltpu.VMEM((c, xl * yl, cells), wide),
            pltpu.VMEM((2 * c * yl, 2 * cells), wide),
        ],
        compiler_params=pltpu.CompilerParams(vmem_limit_bytes=48 * 2**20),
        name="merge_call",
    )(upper, pooled, coefficients, table, mixing, offsets, twice)


def plain_layer(field, coefficients, table, mixing, offsets):
    c, xl, yl, cells = field.shape
    total = jnp.einsum("cnp,nz->cpz", coefficients, table, preferred_element_type=wide)
    total = total.reshape(field.shape)
    total = total + jnp.einsum("cxyz,co->oxyz", field, mixing, preferred_element_type=wide)
    return gelu(total + offsets[:, None, None, None]).astype(narrow)


def plain_pool(upper):
    c, xl, yl, cells = upper.shape
    blocks = upper.astype(wide).reshape(c, xl // 2, 2, yl // 2, 2, cells // 2, 2)
    return blocks.mean(axis=(2, 4, 6)).astype(narrow)


def plain_merge(upper, lower):
    c, xl, yl, cells = upper.shape
    blocks = upper.astype(wide).reshape(c, xl // 2, 2, yl // 2, 2, cells // 2, 2)
    merged = blocks + lower.astype(wide)[:, :, None, :, None, :, None]
    return merged.reshape(upper.shape).astype(narrow)


def on_device(field, spec_fine, mix_fine, bias_fine, spec_coarse, mix_coarse, bias_coarse):
    c, xl, yl, cells = field.shape
    tiled = yl % 16 == 0 and 128 % yl == 0 and (xl * yl) % 128 == 0 and xl % 4 == 0 and 128 % xl == 0
    find = tiled_coefficients if tiled else spectral_coefficients
    found, table = find(field, spec_fine)
    if tiled:
        upper, pooled = upper_call(field, found, table, mix_fine, bias_fine)
    else:
        upper = plain_layer(field, found, table, mix_fine, bias_fine)
        pooled = plain_pool(upper)
    found, table = find(pooled, spec_coarse)
    if tiled:
        return merge_call(upper, pooled, found, table, mix_coarse, bias_coarse)
    return plain_merge(upper, plain_layer(pooled, found, table, mix_coarse, bias_coarse))


def solution(mesh):
    return jax.shard_map(
        on_device,
        mesh=mesh,
        in_specs=(
            P(None, "px", "py", None),
            P(None, None, None, None, "px", "py"),
            P(),
            P(),
            P(None, None, None, None, "px", "py"),
            P(),
            P(),
        ),
        out_specs=P(None, "px", "py", None),
        check_vma=False,
    )
```

profile of v0, /device:TPU:0, one launch (start us, length us, event | category | flops | bytes accessed | tf_op | source)
XLA Modules:
  0.0 292.9 jit_solution(15038214425478768872)
XLA Ops:
  0.7 8.0 %depth_lines.2 = bf16[32,64,512]{2,1,0:T(8,128)(2,1)} custom-call(bf16[64,128]{1,0:T(8,128)(2,1)} %bitcast.215, bf16[32,512,128]{2,1,0:T(8,128)(2,1)} %bitcast.199), custom_call_target="tpu_custom_call" | custom-call | tf_op jit(solution)/shard_map/depth_lines/pallas_call | solution.py:234
  8.7 5.2 %all-to-all-start = ((bf16[4,8,64,512]{3,2,1,0:T(8,128)(2,1)}), bf16[4,8,64,512]{3,2,1,0:T(8,128)(2,1)S(1)}, u32[]{:S(2)}, u32[]{:S(2)}) async-start(bf16[4,8,64,512]{3,2,1,0:T(8,128)(2,1)} %bitcast.200), calls=%async_computation | async-start | bytes 4194304 | tf_op jit(solution)/shard_map/all_to_all | solution.py:45
  14.0 3.5 %select_convert_fusion.3.table = bf16[4,2,128,256]{3,2,1,0:T(8,128)(2,1)} fusion(s32[256]{0:T(256)S(1)} %get-tuple-element.31, s32[256]{0:T(256)S(1)} %get-tuple-element.32, s32[128]{0:T(128)S(1)} %get-tuple-element.38, s32[128]{0:T(128)S(1)} %get-tuple-element.41, s32[4]{0:T(128)S(1)} %iota_multiply_fusion.1, s32[256]{0:T(256)S(1)} %get-tuple-element.29, ...), kind=kLoop, calls=%fused_computation.98 | loop fusion | flops 10485760 | bytes 533520 | tf_op jit(solution)/shard_map/convert_element_type | solution.py:98
  17.4 21.3 %all-to-all-done.d = bf16[4,8,64,512]{3,2,1,0:T(8,128)(2,1)S(1)} async-done(((bf16[4,8,64,512]{3,2,1,0:T(8,128)(2,1)}), bf16[4,8,64,512]{3,2,1,0:T(8,128)(2,1)S(1)}, u32[]{:S(2)}, u32[]{:S(2)}) %all-to-all-start) | async-done | bytes 2097184 | tf_op jit(solution)/shard_map/all_to_all | solution.py:45
  40.0 3.5 %rows_call.2 = bf16[8,8,2,4,512]{4,3,2,1,0:T(4,128)(2,1)} custom-call(bf16[4,8,64,512]{3,2,1,0:T(8,128)(2,1)} %copy-done.5, bf16[4,2,128,256]{3,2,1,0:T(8,128)(2,1)} %select_convert_fusion.3.table), custom_call_target="tpu_custom_call" | custom-call | tf_op jit(solution)/shard_map/rows_call/pallas_call | solution.py:126
  43.6 5.0 %all-to-all-start.1 = ((bf16[8,8,2,4,512]{4,3,2,1,0:T(4,128)(2,1)}), bf16[8,8,2,4,512]{4,3,2,1,0:T(4,128)(2,1)S(1)}, u32[]{:S(2)}, u32[]{:S(2)}) async-start(bf16[8,8,2,4,512]{4,3,2,1,0:T(4,128)(2,1)} %rows_call.2), calls=%async_computation.1 | async-start | bytes 1048576 | tf_op jit(solution)/shard_map/all_to_all | solution.py:45
  49.8 14.1 %all-to-all-done.1 = bf16[8,8,2,4,512]{4,3,2,1,0:T(4,128)(2,1)S(1)} async-done(((bf16[8,8,2,4,512]{4,3,2,1,0:T(4,128)(2,1)}), bf16[8,8,2,4,512]{4,3,2,1,0:T(4,128)(2,1)S(1)}, u32[]{:S(2)}, u32[]{:S(2)}) %all-to-all-start.1) | async-done | bytes 524320 | tf_op jit(solution)/shard_map/all_to_all | solution.py:45
  70.3 5.0 %all-to-all-done.2 = bf16[4,2,8192]{2,1,0:T(2,128)(2,1)S(1)} async-done(((bf16[4,2,8192]{2,1,0:T(2,128)(2,1)}), bf16[4,2,8192]{2,1,0:T(2,128)(2,1)S(1)}, u32[]{:S(2)}, u32[]{:S(2)}) %all-to-all-start.2) | async-done | bytes 131104 | tf_op jit(solution)/shard_map/all_to_all | solution.py:45
  76.0 18.7 %fusion.1 = (bf16[32,32,8,4]{1,3,2,0:T(4,128)(2,1)S(1)}, bf16[32,32,8,4]{1,3,2,0:T(4,128)(2,1)S(1)}) fusion(f32[32,32,8,4]{1,3,2,0:T(4,128)S(1)} %copy.33, f32[32,32,8,4]{1,3,2,0:T(4,128)S(1)} %copy.32, bf16[2,32,32,32,8,4]{3,5,4,2,1,0:T(4,128)(2,1)} %param.8), kind=kLoop, calls=%fused_computation.9 | loop fusion | flops 10420224 | bytes 4587520 | tf_op jit(solution)/shard_map/reduce_sum | solution.py:53
  99.8 5.0 %all-to-all-done.3 = bf16[4,2,8192]{2,1,0:T(2,128)(2,1)S(1)} async-done(((bf16[4,2,8192]{2,1,0:T(2,128)(2,1)}), bf16[4,2,8192]{2,1,0:T(2,128)(2,1)S(1)}, u32[]{:S(2)}, u32[]{:S(2)}) %all-to-all-start.3) | async-done | bytes 131104 | tf_op jit(solution)/shard_map/all_to_all | solution.py:45
  108.4 3.7 %all-to-all-start.4 = ((bf16[8,8,2,4,512]{4,3,2,1,0:T(4,128)(2,1)}), bf16[8,8,2,4,512]{4,3,2,1,0:T(4,128)(2,1)S(1)}, u32[]{:S(2)}, u32[]{:S(2)}) async-start(bf16[8,8,2,4,512]{4,3,2,1,0:T(4,128)(2,1)} %copy.70), calls=%async_computation.4 | async-start | bytes 1048576 | tf_op jit(solution)/shard_map/all_to_all | solution.py:45
  112.4 3.4 %select_convert_fusion.2.table = bf16[2,4,128,256]{3,2,1,0:T(8,128)(2,1)} fusion(s32[128]{0:T(128)S(1)} %get-tuple-element.38, s32[128]{0:T(128)S(1)} %get-tuple-element.41, s32[256]{0:T(256)S(1)} %get-tuple-element.31, s32[256]{0:T(256)S(1)} %get-tuple-element.32, s32[4]{0:T(128)S(1)} %iota_multiply_fusion.1, s32[256]{0:T(256)S(1)} %get-tuple-element.29, ...), kind=kLoop, calls=%fused_computation.97 | loop fusion | flops 10485760 | bytes 533520 | tf_op jit(solution)/shard_map/convert_element_type | solution.py:98
  115.8 11.3 %all-to-all-done.4.b = bf16[8,8,2,4,512]{4,3,2,1,0:T(4,128)(2,1)S(1)} async-done(((bf16[8,8,2,4,512]{4,3,2,1,0:T(4,128)(2,1)}), bf16[8,8,2,4,512]{4,3,2,1,0:T(4,128)(2,1)S(1)}, u32[]{:S(2)}, u32[]{:S(2)}) %all-to-all-start.4) | async-done | bytes 524320 | tf_op jit(solution)/shard_map/all_to_all | solution.py:45
  128.0 3.5 %rows_back_call.2 = bf16[4,8,64,512]{3,2,1,0:T(8,128)(2,1)} custom-call(bf16[8,8,2,4,512]{4,3,2,1,0:T(4,128)(2,1)} %copy-done.7, bf16[2,4,128,256]{3,2,1,0:T(8,128)(2,1)} %select_convert_fusion.2.table), custom_call_target="tpu_custom_call" | custom-call | tf_op jit(solution)/shard_map/rows_back_call/pallas_call | solution.py:166
  131.5 3.6 %all-to-all-start.5 = ((bf16[4,8,64,512]{3,2,1,0:T(8,128)(2,1)}), bf16[4,8,64,512]{3,2,1,0:T(8,128)(2,1)S(1)}, u32[]{:S(2)}, u32[]{:S(2)}) async-start(bf16[4,8,64,512]{3,2,1,0:T(8,128)(2,1)} %rows_back_call.2), calls=%async_computation.5 | async-start | bytes 4194304 | tf_op jit(solution)/shard_map/all_to_all | solution.py:45
  136.6 23.3 %all-to-all-done.5 = bf16[4,8,64,512]{3,2,1,0:T(8,128)(2,1)S(1)} async-done(((bf16[4,8,64,512]{3,2,1,0:T(8,128)(2,1)}), bf16[4,8,64,512]{3,2,1,0:T(8,128)(2,1)S(1)}, u32[]{:S(2)}, u32[]{:S(2)}) %all-to-all-start.5) | async-done | bytes 2097184 | tf_op jit(solution)/shard_map/all_to_all | solution.py:45
  159.9 17.2 %upper_call.1 = (bf16[32,32,16,128]{3,2,1,0:T(8,128)(2,1)}, bf16[32,16,8,64]{3,2,1,0:T(8,128)(2,1)S(1)}) custom-call(bf16[32,32,16,128]{3,2,1,0:T(8,128)(2,1)} %field.1, bf16[32,64,512]{2,1,0:T(8,128)(2,1)S(1)} %bitcast.194, bf16[64,128]{1,0:T(8,128)(2,1)S(1)} %bitcast.197, bf16[512,512]{1,0:T(8,128)(2,1)S(1)} %fusion.25.mixing, ...), custom_call_target="tpu_custom_call" | custom-call | tf_op jit(solution)/shard_map/upper_call/pallas_call | solution.py:302
  178.1 5.9 %depth_lines.3 = bf16[32,64,128]{2,1,0:T(8,128)(2,1)} custom-call(bf16[64,64]{1,0:T(8,128)(2,1)} %bitcast.214, bf16[32,128,64]{2,1,0:T(8,128)(2,1)} %bitcast.195), custom_call_target="tpu_custom_call" | custom-call | tf_op jit(solution)/shard_map/depth_lines/pallas_call | solution.py:234
  183.9 3.5 %all-to-all-start.6 = ((bf16[4,8,64,128]{3,2,1,0:T(8,128)(2,1)}), bf16[4,8,64,128]{3,2,1,0:T(8,128)(2,1)S(1)}, u32[]{:S(2)}, u32[]{:S(2)}) async-start(bf16[4,8,64,128]{3,2,1,0:T(8,128)(2,1)} %bitcast.205), calls=%async_computation.6 | async-start | bytes 1048576 | tf_op jit(solution)/shard_map/all_to_all | solution.py:45
  187.4 5.7 %select_convert_fusion.1.table = bf16[4,2,128,512]{3,2,1,0:T(8,128)(2,1)} fusion(s32[512]{0:T(512)S(1)} %get-tuple-element.51, s32[512]{0:T(512)S(1)} %get-tuple-element.52, s32[128]{0:T(128)S(1)} %get-tuple-element.60, s32[128]{0:T(128)S(1)} %get-tuple-element.61, s32[4]{0:T(128)S(1)} %iota_multiply_fusion, s32[512]{0:T(512)S(1)} %get-tuple-element.49, ...), kind=kLoop, calls=%fused_computation.51 | loop fusion | flops 20971520 | bytes 1064720 | tf_op jit(solution)/shard_map/convert_element_type | solution.py:98
  198.6 3.4 %all-to-all-start.7 = ((bf16[8,8,2,4,256]{4,3,2,1,0:T(4,128)(2,1)}), bf16[8,8,2,4,256]{4,3,2,1,0:T(4,128)(2,1)S(1)}, u32[]{:S(2)}, u32[]{:S(2)}) async-start(bf16[8,8,2,4,256]{4,3,2,1,0:T(4,128)(2,1)} %rows_call.3), calls=%async_computation.7 | async-start | bytes 524288 | tf_op jit(solution)/shard_map/all_to_all | solution.py:45
  203.2 8.4 %all-to-all-done.7 = bf16[8,8,2,4,256]{4,3,2,1,0:T(4,128)(2,1)S(1)} async-done(((bf16[8,8,2,4,256]{4,3,2,1,0:T(4,128)(2,1)}), bf16[8,8,2,4,256]{4,3,2,1,0:T(4,128)(2,1)S(1)}, u32[]{:S(2)}, u32[]{:S(2)}) %all-to-all-start.7) | async-done | bytes 262176 | tf_op jit(solution)/shard_map/all_to_all | solution.py:45
  214.0 3.5 %all-to-all-start.8 = ((bf16[4,2,8192]{2,1,0:T(2,128)(2,1)}), bf16[4,2,8192]{2,1,0:T(2,128)(2,1)S(1)}, u32[]{:S(2)}, u32[]{:S(2)}) async-start(bf16[4,2,8192]{2,1,0:T(2,128)(2,1)} %reshape.1106), calls=%async_computation.8 | async-start | bytes 262144 | tf_op jit(solution)/shard_map/all_to_all | solution.py:45
  217.5 5.9 %select_convert_fusion.table = bf16[2,4,256,256]{3,2,1,0:T(8,128)(2,1)} fusion(s32[256]{0:T(256)S(1)} %get-tuple-element.31, s32[256]{0:T(256)S(1)} %get-tuple-element.32, s32[256]{0:T(256)S(1)} %get-tuple-element.66, s32[256]{0:T(256)S(1)} %get-tuple-element.67, s32[4]{0:T(128)S(1)} %iota_multiply_fusion, s32[256]{0:T(256)S(1)} %get-tuple-element.29, ...), kind=kLoop, calls=%fused_computation.50 | loop fusion | flops 20971520 | bytes 1060112 | tf_op jit(solution)/shard_map/convert_element_type | solution.py:98
  224.2 18.7 %fusion.5 = (bf16[32,32,8,4]{1,3,2,0:T(4,128)(2,1)S(1)}, bf16[32,32,8,4]{1,3,2,0:T(4,128)(2,1)S(1)}) fusion(f32[32,32,8,4]{1,3,2,0:T(4,128)S(1)} %copy.43, f32[32,32,8,4]{1,3,2,0:T(4,128)S(1)} %copy.42, bf16[2,32,32,32,8,4]{3,5,4,2,1,0:T(4,128)(2,1)} %param.11), kind=kLoop, calls=%fused_computation.13 | loop fusion | flops 10420224 | bytes 4587520 | tf_op jit(solution)/shard_map/reduce_sum | solution.py:53
  244.6 3.9 %all-to-all-start.9 = ((bf16[4,2,8192]{2,1,0:T(2,128)(2,1)}), bf16[4,2,8192]{2,1,0:T(2,128)(2,1)S(1)}, u32[]{:S(2)}, u32[]{:S(2)}) async-start(bf16[4,2,8192]{2,1,0:T(2,128)(2,1)} %reshape.1108), calls=%async_computation.9 | async-start | bytes 262144 | tf_op jit(solution)/shard_map/all_to_all | solution.py:45
  248.5 5.0 %all-to-all-done.9 = bf16[4,2,8192]{2,1,0:T(2,128)(2,1)S(1)} async-done(((bf16[4,2,8192]{2,1,0:T(2,128)(2,1)}), bf16[4,2,8192]{2,1,0:T(2,128)(2,1)S(1)}, u32[]{:S(2)}, u32[]{:S(2)}) %all-to-all-start.9) | async-done | bytes 131104 | tf_op jit(solution)/shard_map/all_to_all | solution.py:45
  255.8 3.5 %all-to-all-start.10 = ((bf16[8,8,2,4,256]{4,3,2,1,0:T(4,128)(2,1)}), bf16[8,8,2,4,256]{4,3,2,1,0:T(4,128)(2,1)S(1)}, u32[]{:S(2)}, u32[]{:S(2)}) async-start(bf16[8,8,2,4,256]{4,3,2,1,0:T(4,128)(2,1)} %copy.79), calls=%async_computation.10 | async-start | bytes 524288 | tf_op jit(solution)/shard_map/all_to_all | solution.py:45
  259.5 9.5 %all-to-all-done.10.b = bf16[8,8,2,4,256]{4,3,2,1,0:T(4,128)(2,1)S(1)} async-done(((bf16[8,8,2,4,256]{4,3,2,1,0:T(4,128)(2,1)}), bf16[8,8,2,4,256]{4,3,2,1,0:T(4,128)(2,1)S(1)}, u32[]{:S(2)}, u32[]{:S(2)}) %all-to-all-start.10) | async-done | bytes 262176 | tf_op jit(solution)/shard_map/all_to_all | solution.py:45
  272.4 3.5 %all-to-all-start.11 = ((bf16[4,8,64,128]{3,2,1,0:T(8,128)(2,1)}), bf16[4,8,64,128]{3,2,1,0:T(8,128)(2,1)S(1)}, u32[]{:S(2)}, u32[]{:S(2)}) async-start(bf16[4,8,64,128]{3,2,1,0:T(8,128)(2,1)} %rows_back_call.3), calls=%async_computation.11 | async-start | bytes 1048576 | tf_op jit(solution)/shard_map/all_to_all | solution.py:45
  276.5 7.3 %all-to-all-done.11 = bf16[4,8,64,128]{3,2,1,0:T(8,128)(2,1)S(1)} async-done(((bf16[4,8,64,128]{3,2,1,0:T(8,128)(2,1)}), bf16[4,8,64,128]{3,2,1,0:T(8,128)(2,1)S(1)}, u32[]{:S(2)}, u32[]{:S(2)}) %all-to-all-start.11) | async-done | bytes 524320 | tf_op jit(solution)/shard_map/all_to_all | solution.py:45
  286.0 6.9 %merge_call.1 = bf16[32,32,16,128]{3,2,1,0:T(8,128)(2,1)} custom-call(bf16[32,32,16,128]{3,2,1,0:T(8,128)(2,1)S(1)} %copy-done.4, bf16[32,16,8,64]{3,2,1,0:T(8,128)(2,1)S(1)} %copy-done.3, bf16[32,64,128]{2,1,0:T(8,128)(2,1)S(1)} %bitcast.196, bf16[64,64]{1,0:T(8,128)(2,1)S(1)} %bitcast.198, bf16[256,256]{1,0:T(8,128)(2,1)S(1)} %fusion.34.mixing, ...), custom_call_target="tpu_custom_call" | custom-call | tf_op jit(solution)/shard_map/merge_call/pallas_call | solution.py:359
  (111 shorter events, 42.5 us)
Async XLA Ops:
  0.0 136.0 %copy-start = (bf16[32,32]{1,0:T(8,128)(2,1)S(1)}, bf16[32,32]{1,0:T(8,128)(2,1)}, u32[]{:S(2)}) copy-start(bf16[32,32]{1,0:T(8,128)(2,1)} %param.9) | copy-start | bytes 6148
  8.7 30.1 %all-to-all-start = ((bf16[4,8,64,512]{3,2,1,0:T(8,128)(2,1)}), bf16[4,8,64,512]{3,2,1,0:T(8,128)(2,1)S(1)}, u32[]{:S(2)}, u32[]{:S(2)}) async-start(bf16[4,8,64,512]{3,2,1,0:T(8,128)(2,1)} %bitcast.200), calls=%async_computation | async-start | bytes 4194304 | tf_op jit(solution)/shard_map/all_to_all | solution.py:45
  38.7 1.3 copy-start.5
  43.6 20.4 %all-to-all-start.1 = ((bf16[8,8,2,4,512]{4,3,2,1,0:T(4,128)(2,1)}), bf16[8,8,2,4,512]{4,3,2,1,0:T(4,128)(2,1)S(1)}, u32[]{:S(2)}, u32[]{:S(2)}) async-start(bf16[8,8,2,4,512]{4,3,2,1,0:T(4,128)(2,1)} %rows_call.2), calls=%async_computation.1 | async-start | bytes 1048576 | tf_op jit(solution)/shard_map/all_to_all | solution.py:45
  66.9 8.3 %all-to-all-start.2 = ((bf16[4,2,8192]{2,1,0:T(2,128)(2,1)}), bf16[4,2,8192]{2,1,0:T(2,128)(2,1)S(1)}, u32[]{:S(2)}, u32[]{:S(2)}) async-start(bf16[4,2,8192]{2,1,0:T(2,128)(2,1)} %reshape.1102), calls=%async_computation.2 | async-start | bytes 262144 | tf_op jit(solution)/shard_map/all_to_all | solution.py:45
  96.4 8.3 %all-to-all-start.3 = ((bf16[4,2,8192]{2,1,0:T(2,128)(2,1)}), bf16[4,2,8192]{2,1,0:T(2,128)(2,1)S(1)}, u32[]{:S(2)}, u32[]{:S(2)}) async-start(bf16[4,2,8192]{2,1,0:T(2,128)(2,1)} %reshape.1104), calls=%async_computation.3 | async-start | bytes 262144 | tf_op jit(solution)/shard_map/all_to_all | solution.py:45
  105.8 6.3 %copy-start.9 = (f32[32]{0:T(128)S(1)}, f32[32]{0:T(128)}, u32[]{:S(2)}) copy-start(f32[32]{0:T(128)} %param.10) | copy-start | bytes 388
  108.4 18.8 %all-to-all-start.4 = ((bf16[8,8,2,4,512]{4,3,2,1,0:T(4,128)(2,1)}), bf16[8,8,2,4,512]{4,3,2,1,0:T(4,128)(2,1)S(1)}, u32[]{:S(2)}, u32[]{:S(2)}) async-start(bf16[8,8,2,4,512]{4,3,2,1,0:T(4,128)(2,1)} %copy.70), calls=%async_computation.4 | async-start | bytes 1048576 | tf_op jit(solution)/shard_map/all_to_all | solution.py:45
  127.1 0.8 copy-start.7
  131.5 28.4 %all-to-all-start.5 = ((bf16[4,8,64,512]{3,2,1,0:T(8,128)(2,1)}), bf16[4,8,64,512]{3,2,1,0:T(8,128)(2,1)S(1)}, u32[]{:S(2)}, u32[]{:S(2)}) async-start(bf16[4,8,64,512]{3,2,1,0:T(8,128)(2,1)} %rows_back_call.2), calls=%async_computation.5 | async-start | bytes 4194304 | tf_op jit(solution)/shard_map/all_to_all | solution.py:45
  177.1 1.0 copy-start.2
  183.9 11.0 %all-to-all-start.6 = ((bf16[4,8,64,128]{3,2,1,0:T(8,128)(2,1)}), bf16[4,8,64,128]{3,2,1,0:T(8,128)(2,1)S(1)}, u32[]{:S(2)}, u32[]{:S(2)}) async-start(bf16[4,8,64,128]{3,2,1,0:T(8,128)(2,1)} %bitcast.205), calls=%async_computation.6 | async-start | bytes 1048576 | tf_op jit(solution)/shard_map/all_to_all | solution.py:45
  194.9 0.8 copy-start.6
  198.6 13.1 %all-to-all-start.7 = ((bf16[8,8,2,4,256]{4,3,2,1,0:T(4,128)(2,1)}), bf16[8,8,2,4,256]{4,3,2,1,0:T(4,128)(2,1)S(1)}, u32[]{:S(2)}, u32[]{:S(2)}) async-start(bf16[8,8,2,4,256]{4,3,2,1,0:T(4,128)(2,1)} %rows_call.3), calls=%async_computation.7 | async-start | bytes 524288 | tf_op jit(solution)/shard_map/all_to_all | solution.py:45
  214.0 9.5 %all-to-all-start.8 = ((bf16[4,2,8192]{2,1,0:T(2,128)(2,1)}), bf16[4,2,8192]{2,1,0:T(2,128)(2,1)S(1)}, u32[]{:S(2)}, u32[]{:S(2)}) async-start(bf16[4,2,8192]{2,1,0:T(2,128)(2,1)} %reshape.1106), calls=%async_computation.8 | async-start | bytes 262144 | tf_op jit(solution)/shard_map/all_to_all | solution.py:45
  244.6 8.9 %all-to-all-start.9 = ((bf16[4,2,8192]{2,1,0:T(2,128)(2,1)}), bf16[4,2,8192]{2,1,0:T(2,128)(2,1)S(1)}, u32[]{:S(2)}, u32[]{:S(2)}) async-start(bf16[4,2,8192]{2,1,0:T(2,128)(2,1)} %reshape.1108), calls=%async_computation.9 | async-start | bytes 262144 | tf_op jit(solution)/shard_map/all_to_all | solution.py:45
  255.0 20.9 %copy-start.10 = (f32[32]{0:T(128)S(1)}, f32[32]{0:T(128)}, u32[]{:S(2)}) copy-start(f32[32]{0:T(128)} %param.13) | copy-start | bytes 388
  255.0 21.1 %copy-start.11 = (bf16[32,32]{1,0:T(8,128)(2,1)S(1)}, bf16[32,32]{1,0:T(8,128)(2,1)}, u32[]{:S(2)}) copy-start(bf16[32,32]{1,0:T(8,128)(2,1)} %param.12) | copy-start | bytes 6148
  255.8 27.9 %copy-start.3 = (bf16[32,16,8,64]{3,2,1,0:T(8,128)(2,1)S(1)}, bf16[32,16,8,64]{3,2,1,0:T(8,128)(2,1)}, u32[]{:S(2)}) copy-start(bf16[32,16,8,64]{3,2,1,0:T(8,128)(2,1)} %copy-done.2) | copy-start | bytes 1572868
  255.8 13.2 %all-to-all-start.10 = ((bf16[8,8,2,4,256]{4,3,2,1,0:T(4,128)(2,1)}), bf16[8,8,2,4,256]{4,3,2,1,0:T(4,128)(2,1)S(1)}, u32[]{:S(2)}, u32[]{:S(2)}) async-start(bf16[8,8,2,4,256]{4,3,2,1,0:T(4,128)(2,1)} %copy.79), calls=%async_computation.10 | async-start | bytes 524288 | tf_op jit(solution)/shard_map/all_to_all | solution.py:45
  269.0 0.7 copy-start.8
  272.4 11.4 %all-to-all-start.11 = ((bf16[4,8,64,128]{3,2,1,0:T(8,128)(2,1)}), bf16[4,8,64,128]{3,2,1,0:T(8,128)(2,1)S(1)}, u32[]{:S(2)}, u32[]{:S(2)}) async-start(bf16[4,8,64,128]{3,2,1,0:T(8,128)(2,1)} %rows_back_call.3), calls=%async_computation.11 | async-start | bytes 1048576 | tf_op jit(solution)/shard_map/all_to_all | solution.py:45
  283.8 2.2 copy-start.4
  286.0 6.9 %copy-start.1 = (bf16[32,32]{1,0:T(8,128)(2,1)S(1)}, bf16[32,32]{1,0:T(8,128)(2,1)}, u32[]{:S(2)}) copy-start(bf16[32,32]{1,0:T(8,128)(2,1)} %param.9) | copy-start | bytes 6148
where the time goes:
time: 294 us; the launch traced here: 293 us
  waiting for transfers between devices  112 us (38%)
  other arithmetic  60.9 us (21%)
  Pallas kernels  50.5 us (17%)
  starting transfers between devices  45.5 us (15%)
  local copies, waits for them, and re-layouts  19.8 us (7%)
  matrix products  3.63 us (1%)
    all_to_all x12, waiting for transfers between devices, swap(): return lax.all_to_all(value, axis, split_axis=0, concat_axis=0)  112 us
    all_to_all x12, starting transfers between devices, swap(): return lax.all_to_all(value, axis, split_axis=0, concat_axis=0)  45.5 us
    reduce_sum x2, other arithmetic, mix_modes(): real = (mr * wr - mi * wi).sum(0)  37.3 us
    convert_element_type x4, other arithmetic, line_tables(): return jnp.where(same, value, 0.0).astype(narrow)  18.5 us
    pallas_call x1, Pallas kernels, upper_call(): pl.pallas_call(upper_kernel, out_shape=(jax.ShapeDtypeStruct(field.shape,...  17.2 us
    pallas_call x2, Pallas kernels, depth_lines(): pl.pallas_call(functools.partial(depth_kernel, yl), out_shape=jax.ShapeDt...  13.8 us
    unnamed x32, local copies, waits for them, and re-layouts  12.7 us
    pallas_call x1, Pallas kernels, merge_call(): pl.pallas_call(merge_kernel, out_shape=jax.ShapeDtypeStruct(upper.shape,...  6.92 us
  transfers between devices with their start and end apart: 12, of which 11 were waited for; matrix products, arithmetic and copies ran while one was open for 8% of the time, Pallas kernels for 0%

commit v1 on v0

--- a/solution.py
+++ b/solution.py
@@ -122,7 +122,7 @@
     take, give = table.shape[2], table.shape[3] // 2
     width = points // take * give
     kl = both // 2 // groups
-    cs = 4 if cb % 4 == 0 else 1
+    cs = 2 if cb % 2 == 0 else 1
     return pl.pallas_call(
         rows_kernel,
         out_shape=jax.ShapeDtypeStruct((groups, cb, 2, kl, width), narrow),
@@ -162,7 +162,7 @@
     take, give = table.shape[2], table.shape[3] // 2
     points = width // take * give
     kz = groups * kl
-    cs = 4 if cb % 4 == 0 else 1
+    cs = 2 if cb % 2 == 0 else 1
     return pl.pallas_call(
         rows_back_kernel,
         out_shape=jax.ShapeDtypeStruct((blocks, cb, 2 * kz, points), narrow),
@@ -230,7 +230,7 @@
 
 def depth_lines(lines, table, yl=0):
     c, points, cells = lines.shape
-    step = 4 if c % 4 == 0 else 1
+    step = 2 if c % 2 == 0 else 1
     return pl.pallas_call(
         functools.partial(depth_kernel, yl),
         out_shape=jax.ShapeDtypeStruct((c, table.shape[0], points), narrow),

time: 294 us -> 308 us (1.048)
  Pallas kernels: 50.5 us -> 63 us
    pallas_call x2, Pallas kernels: 13.8 us -> 21.8 us  [depth_lines(): pl.pallas_call(functools.partial(depth_kernel, yl), out_shape=jax.ShapeDt...]
where the time goes in v1:
time: 308 us; the launch traced here: 305 us
  waiting for transfers between devices  112 us (36%)
  Pallas kernels  63 us (20%)
  other arithmetic  60.9 us (20%)
  starting transfers between devices  45.5 us (15%)
  local copies, waits for them, and re-layouts  19.8 us (6%)
  matrix products  3.63 us (1%)
    all_to_all x12, waiting for transfers between devices, swap(): return lax.all_to_all(value, axis, split_axis=0, concat_axis=0)  112 us
    all_to_all x12, starting transfers between devices, swap(): return lax.all_to_all(value, axis, split_axis=0, concat_axis=0)  45.5 us
    reduce_sum x2, other arithmetic, mix_modes(): real = (mr * wr - mi * wi).sum(0)  37.3 us
    pallas_call x2, Pallas kernels, depth_lines(): pl.pallas_call(functools.partial(depth_kernel, yl), out_shape=jax.ShapeDt...  21.8 us
    convert_element_type x4, other arithmetic, line_tables(): return jnp.where(same, value, 0.0).astype(narrow)  18.5 us
    pallas_call x1, Pallas kernels, upper_call(): pl.pallas_call(upper_kernel, out_shape=(jax.ShapeDtypeStruct(field.shape,...  17.2 us
    unnamed x32, local copies, waits for them, and re-layouts  12.7 us
    pallas_call x2, Pallas kernels, rows_call(): pl.pallas_call(rows_kernel, out_shape=jax.ShapeDtypeStruct((groups, cb, 2...  8.58 us
  transfers between devices with their start and end apart: 12, of which 11 were waited for; matrix products, arithmetic and copies ran while one was open for 8% of the time, Pallas kernels for 0%

profile of v1, /device:TPU:0, one launch (start us, length us, event | category | flops | bytes accessed | tf_op | source)
XLA Modules:
  0.0 305.4 jit_solution(17654740757054678374)
XLA Ops:
  0.7 12.0 %depth_lines.2 = bf16[32,64,512]{2,1,0:T(8,128)(2,1)} custom-call(bf16[64,128]{1,0:T(8,128)(2,1)} %bitcast.215, bf16[32,512,128]{2,1,0:T(8,128)(2,1)} %bitcast.199), custom_call_target="tpu_custom_call" | custom-call | tf_op jit(solution)/shard_map/depth_lines/pallas_call | solution.py:234
  12.7 5.2 %all-to-all-start = ((bf16[4,8,64,512]{3,2,1,0:T(8,128)(2,1)}), bf16[4,8,64,512]{3,2,1,0:T(8,128)(2,1)S(1)}, u32[]{:S(2)}, u32[]{:S(2)}) async-start(bf16[4,8,64,512]{3,2,1,0:T(8,128)(2,1)} %bitcast.200), calls=%async_computation | async-start | bytes 4194304 | tf_op jit(solution)/shard_map/all_to_all | solution.py:45
  18.0 3.5 %select_convert_fusion.3.table = bf16[4,2,128,256]{3,2,1,0:T(8,128)(2,1)} fusion(s32[256]{0:T(256)S(1)} %get-tuple-element.31, s32[256]{0:T(256)S(1)} %get-tuple-element.32, s32[128]{0:T(128)S(1)} %get-tuple-element.38, s32[128]{0:T(128)S(1)} %get-tuple-element.41, s32[4]{0:T(128)S(1)} %iota_multiply_fusion.1, s32[256]{0:T(256)S(1)} %get-tuple-element.29, ...), kind=kLoop, calls=%fused_computation.98 | loop fusion | flops 10485760 | bytes 533520 | tf_op jit(solution)/shard_map/convert_element_type | solution.py:98
  21.5 21.3 %all-to-all-done.d = bf16[4,8,64,512]{3,2,1,0:T(8,128)(2,1)S(1)} async-done(((bf16[4,8,64,512]{3,2,1,0:T(8,128)(2,1)}), bf16[4,8,64,512]{3,2,1,0:T(8,128)(2,1)S(1)}, u32[]{:S(2)}, u32[]{:S(2)}) %all-to-all-start) | async-done | bytes 2097184 | tf_op jit(solution)/shard_map/all_to_all | solution.py:45
  44.1 4.5 %rows_call.2 = bf16[8,8,2,4,512]{4,3,2,1,0:T(4,128)(2,1)} custom-call(bf16[4,8,64,512]{3,2,1,0:T(8,128)(2,1)} %copy-done.5, bf16[4,2,128,256]{3,2,1,0:T(8,128)(2,1)} %select_convert_fusion.3.table), custom_call_target="tpu_custom_call" | custom-call | tf_op jit(solution)/shard_map/rows_call/pallas_call | solution.py:126
  48.5 5.0 %all-to-all-start.1 = ((bf16[8,8,2,4,512]{4,3,2,1,0:T(4,128)(2,1)}), bf16[8,8,2,4,512]{4,3,2,1,0:T(4,128)(2,1)S(1)}, u32[]{:S(2)}, u32[]{:S(2)}) async-start(bf16[8,8,2,4,512]{4,3,2,1,0:T(4,128)(2,1)} %rows_call.2), calls=%async_computation.1 | async-start | bytes 1048576 | tf_op jit(solution)/shard_map/all_to_all | solution.py:45
  54.8 14.1 %all-to-all-done.1 = bf16[8,8,2,4,512]{4,3,2,1,0:T(4,128)(2,1)S(1)} async-done(((bf16[8,8,2,4,512]{4,3,2,1,0:T(4,128)(2,1)}), bf16[8,8,2,4,512]{4,3,2,1,0:T(4,128)(2,1)S(1)}, u32[]{:S(2)}, u32[]{:S(2)}) %all-to-all-start.1) | async-done | bytes 524320 | tf_op jit(solution)/shard_map/all_to_all | solution.py:45
  75.2 5.0 %all-to-all-done.2 = bf16[4,2,8192]{2,1,0:T(2,128)(2,1)S(1)} async-done(((bf16[4,2,8192]{2,1,0:T(2,128)(2,1)}), bf16[4,2,8192]{2,1,0:T(2,128)(2,1)S(1)}, u32[]{:S(2)}, u32[]{:S(2)}) %all-to-all-start.2) | async-done | bytes 131104 | tf_op jit(solution)/shard_map/all_to_all | solution.py:45
  81.0 18.7 %fusion.1 = (bf16[32,32,8,4]{1,3,2,0:T(4,128)(2,1)S(1)}, bf16[32,32,8,4]{1,3,2,0:T(4,128)(2,1)S(1)}) fusion(f32[32,32,8,4]{1,3,2,0:T(4,128)S(1)} %copy.33, f32[32,32,8,4]{1,3,2,0:T(4,128)S(1)} %copy.32, bf16[2,32,32,32,8,4]{3,5,4,2,1,0:T(4,128)(2,1)} %param.8), kind=kLoop, calls=%fused_computation.9 | loop fusion | flops 10420224 | bytes 4587520 | tf_op jit(solution)/shard_map/reduce_sum | solution.py:53
  104.8 5.0 %all-to-all-done.3 = bf16[4,2,8192]{2,1,0:T(2,128)(2,1)S(1)} async-done(((bf16[4,2,8192]{2,1,0:T(2,128)(2,1)}), bf16[4,2,8192]{2,1,0:T(2,128)(2,1)S(1)}, u32[]{:S(2)}, u32[]{:S(2)}) %all-to-all-start.3) | async-done | bytes 131104 | tf_op jit(solution)/shard_map/all_to_all | solution.py:45
  113.4 3.7 %all-to-all-start.4 = ((bf16[8,8,2,4,512]{4,3,2,1,0:T(4,128)(2,1)}), bf16[8,8,2,4,512]{4,3,2,1,0:T(4,128)(2,1)S(1)}, u32[]{:S(2)}, u32[]{:S(2)}) async-start(bf16[8,8,2,4,512]{4,3,2,1,0:T(4,128)(2,1)} %copy.70), calls=%async_computation.4 | async-start | bytes 1048576 | tf_op jit(solution)/shard_map/all_to_all | solution.py:45
  120.8 11.3 %all-to-all-done.4.b = bf16[8,8,2,4,512]{4,3,2,1,0:T(4,128)(2,1)S(1)} async-done(((bf16[8,8,2,4,512]{4,3,2,1,0:T(4,128)(2,1)}), bf16[8,8,2,4,512]{4,3,2,1,0:T(4,128)(2,1)S(1)}, u32[]{:S(2)}, u32[]{:S(2)}) %all-to-all-start.4) | async-done | bytes 524320 | tf_op jit(solution)/shard_map/all_to_all | solution.py:45
  132.9 4.5 %rows_back_call.2 = bf16[4,8,64,512]{3,2,1,0:T(8,128)(2,1)} custom-call(bf16[8,8,2,4,512]{4,3,2,1,0:T(4,128)(2,1)} %copy-done.7, bf16[2,4,128,256]{3,2,1,0:T(8,128)(2,1)} %select_convert_fusion.2.table), custom_call_target="tpu_custom_call" | custom-call | tf_op jit(solution)/shard_map/rows_back_call/pallas_call | solution.py:166
  137.4 3.6 %all-to-all-start.5 = ((bf16[4,8,64,512]{3,2,1,0:T(8,128)(2,1)}), bf16[4,8,64,512]{3,2,1,0:T(8,128)(2,1)S(1)}, u32[]{:S(2)}, u32[]{:S(2)}) async-start(bf16[4,8,64,512]{3,2,1,0:T(8,128)(2,1)} %rows_back_call.2), calls=%async_computation.5 | async-start | bytes 4194304 | tf_op jit(solution)/shard_map/all_to_all | solution.py:45
  142.6 23.3 %all-to-all-done.5 = bf16[4,8,64,512]{3,2,1,0:T(8,128)(2,1)S(1)} async-done(((bf16[4,8,64,512]{3,2,1,0:T(8,128)(2,1)}), bf16[4,8,64,512]{3,2,1,0:T(8,128)(2,1)S(1)}, u32[]{:S(2)}, u32[]{:S(2)}) %all-to-all-start.5) | async-done | bytes 2097184 | tf_op jit(solution)/shard_map/all_to_all | solution.py:45
  165.9 17.2 %upper_call.1 = (bf16[32,32,16,128]{3,2,1,0:T(8,128)(2,1)}, bf16[32,16,8,64]{3,2,1,0:T(8,128)(2,1)S(1)}) custom-call(bf16[32,32,16,128]{3,2,1,0:T(8,128)(2,1)} %field.1, bf16[32,64,512]{2,1,0:T(8,128)(2,1)S(1)} %bitcast.194, bf16[64,128]{1,0:T(8,128)(2,1)S(1)} %bitcast.197, bf16[512,512]{1,0:T(8,128)(2,1)S(1)} %fusion.25.mixing, ...), custom_call_target="tpu_custom_call" | custom-call | tf_op jit(solution)/shard_map/upper_call/pallas_call | solution.py:302
  184.0 9.8 %depth_lines.3 = bf16[32,64,128]{2,1,0:T(8,128)(2,1)} custom-call(bf16[64,64]{1,0:T(8,128)(2,1)} %bitcast.214, bf16[32,128,64]{2,1,0:T(8,128)(2,1)} %bitcast.195), custom_call_target="tpu_custom_call" | custom-call | tf_op jit(solution)/shard_map/depth_lines/pallas_call | solution.py:234
  193.8 3.5 %all-to-all-start.6 = ((bf16[4,8,64,128]{3,2,1,0:T(8,128)(2,1)}), bf16[4,8,64,128]{3,2,1,0:T(8,128)(2,1)S(1)}, u32[]{:S(2)}, u32[]{:S(2)}) async-start(bf16[4,8,64,128]{3,2,1,0:T(8,128)(2,1)} %bitcast.205), calls=%async_computation.6 | async-start | bytes 1048576 | tf_op jit(solution)/shard_map/all_to_all | solution.py:45
  197.3 5.7 %select_convert_fusion.1.table = bf16[4,2,128,512]{3,2,1,0:T(8,128)(2,1)} fusion(s32[512]{0:T(512)S(1)} %get-tuple-element.51, s32[512]{0:T(512)S(1)} %get-tuple-element.52, s32[128]{0:T(128)S(1)} %get-tuple-element.60, s32[128]{0:T(128)S(1)} %get-tuple-element.61, s32[4]{0:T(128)S(1)} %iota_multiply_fusion, s32[512]{0:T(512)S(1)} %get-tuple-element.49, ...), kind=kLoop, calls=%fused_computation.51 | loop fusion | flops 20971520 | bytes 1064720 | tf_op jit(solution)/shard_map/convert_element_type | solution.py:98
  205.6 4.1 %rows_call.3 = bf16[8,8,2,4,256]{4,3,2,1,0:T(4,128)(2,1)} custom-call(bf16[4,8,64,128]{3,2,1,0:T(8,128)(2,1)} %copy-done.6, bf16[4,2,128,512]{3,2,1,0:T(8,128)(2,1)} %select_convert_fusion.1.table), custom_call_target="tpu_custom_call" | custom-call | tf_op jit(solution)/shard_map/rows_call/pallas_call | solution.py:126
  214.3 8.4 %all-to-all-done.7 = bf16[8,8,2,4,256]{4,3,2,1,0:T(4,128)(2,1)S(1)} async-done(((bf16[8,8,2,4,256]{4,3,2,1,0:T(4,128)(2,1)}), bf16[8,8,2,4,256]{4,3,2,1,0:T(4,128)(2,1)S(1)}, u32[]{:S(2)}, u32[]{:S(2)}) %all-to-all-start.7) | async-done | bytes 262176 | tf_op jit(solution)/shard_map/all_to_all | solution.py:45
  225.1 3.5 %all-to-all-start.8 = ((bf16[4,2,8192]{2,1,0:T(2,128)(2,1)}), bf16[4,2,8192]{2,1,0:T(2,128)(2,1)S(1)}, u32[]{:S(2)}, u32[]{:S(2)}) async-start(bf16[4,2,8192]{2,1,0:T(2,128)(2,1)} %reshape.1106), calls=%async_computation.8 | async-start | bytes 262144 | tf_op jit(solution)/shard_map/all_to_all | solution.py:45
  228.6 5.9 %select_convert_fusion.table = bf16[2,4,256,256]{3,2,1,0:T(8,128)(2,1)} fusion(s32[256]{0:T(256)S(1)} %get-tuple-element.31, s32[256]{0:T(256)S(1)} %get-tuple-element.32, s32[256]{0:T(256)S(1)} %get-tuple-element.66, s32[256]{0:T(256)S(1)} %get-tuple-element.67, s32[4]{0:T(128)S(1)} %iota_multiply_fusion, s32[256]{0:T(256)S(1)} %get-tuple-element.29, ...), kind=kLoop, calls=%fused_computation.50 | loop fusion | flops 20971520 | bytes 1060112 | tf_op jit(solution)/shard_map/convert_element_type | solution.py:98
  235.3 18.7 %fusion.5 = (bf16[32,32,8,4]{1,3,2,0:T(4,128)(2,1)S(1)}, bf16[32,32,8,4]{1,3,2,0:T(4,128)(2,1)S(1)}) fusion(f32[32,32,8,4]{1,3,2,0:T(4,128)S(1)} %copy.43, f32[32,32,8,4]{1,3,2,0:T(4,128)S(1)} %copy.42, bf16[2,32,32,32,8,4]{3,5,4,2,1,0:T(4,128)(2,1)} %param.11), kind=kLoop, calls=%fused_computation.13 | loop fusion | flops 10420224 | bytes 4587520 | tf_op jit(solution)/shard_map/reduce_sum | solution.py:53
  255.8 3.9 %all-to-all-start.9 = ((bf16[4,2,8192]{2,1,0:T(2,128)(2,1)}), bf16[4,2,8192]{2,1,0:T(2,128)(2,1)S(1)}, u32[]{:S(2)}, u32[]{:S(2)}) async-start(bf16[4,2,8192]{2,1,0:T(2,128)(2,1)} %reshape.1108), calls=%async_computation.9 | async-start | bytes 262144 | tf_op jit(solution)/shard_map/all_to_all | solution.py:45
  259.7 5.0 %all-to-all-done.9 = bf16[4,2,8192]{2,1,0:T(2,128)(2,1)S(1)} async-done(((bf16[4,2,8192]{2,1,0:T(2,128)(2,1)}), bf16[4,2,8192]{2,1,0:T(2,128)(2,1)S(1)}, u32[]{:S(2)}, u32[]{:S(2)}) %all-to-all-start.9) | async-done | bytes 131104 | tf_op jit(solution)/shard_map/all_to_all | solution.py:45
  267.0 3.5 %all-to-all-start.10 = ((bf16[8,8,2,4,256]{4,3,2,1,0:T(4,128)(2,1)}), bf16[8,8,2,4,256]{4,3,2,1,0:T(4,128)(2,1)S(1)}, u32[]{:S(2)}, u32[]{:S(2)}) async-start(bf16[8,8,2,4,256]{4,3,2,1,0:T(4,128)(2,1)} %copy.79), calls=%async_computation.10 | async-start | bytes 524288 | tf_op jit(solution)/shard_map/all_to_all | solution.py:45
  270.6 9.5 %all-to-all-done.10.b = bf16[8,8,2,4,256]{4,3,2,1,0:T(4,128)(2,1)S(1)} async-done(((bf16[8,8,2,4,256]{4,3,2,1,0:T(4,128)(2,1)}), bf16[8,8,2,4,256]{4,3,2,1,0:T(4,128)(2,1)S(1)}, u32[]{:S(2)}, u32[]{:S(2)}) %all-to-all-start.10) | async-done | bytes 262176 | tf_op jit(solution)/shard_map/all_to_all | solution.py:45
  280.9 4.0 %rows_back_call.3 = bf16[4,8,64,128]{3,2,1,0:T(8,128)(2,1)} custom-call(bf16[8,8,2,4,256]{4,3,2,1,0:T(4,128)(2,1)} %copy-done.8, bf16[2,4,256,256]{3,2,1,0:T(8,128)(2,1)} %select_convert_fusion.table), custom_call_target="tpu_custom_call" | custom-call | tf_op jit(solution)/shard_map/rows_back_call/pallas_call | solution.py:166
  284.9 3.5 %all-to-all-start.11 = ((bf16[4,8,64,128]{3,2,1,0:T(8,128)(2,1)}), bf16[4,8,64,128]{3,2,1,0:T(8,128)(2,1)S(1)}, u32[]{:S(2)}, u32[]{:S(2)}) async-start(bf16[4,8,64,128]{3,2,1,0:T(8,128)(2,1)} %rows_back_call.3), calls=%async_computation.11 | async-start | bytes 1048576 | tf_op jit(solution)/shard_map/all_to_all | solution.py:45
  289.0 7.3 %all-to-all-done.11 = bf16[4,8,64,128]{3,2,1,0:T(8,128)(2,1)S(1)} async-done(((bf16[4,8,64,128]{3,2,1,0:T(8,128)(2,1)}), bf16[4,8,64,128]{3,2,1,0:T(8,128)(2,1)S(1)}, u32[]{:S(2)}, u32[]{:S(2)}) %all-to-all-start.11) | async-done | bytes 524320 | tf_op jit(solution)/shard_map/all_to_all | solution.py:45
  298.5 6.9 %merge_call.1 = bf16[32,32,16,128]{3,2,1,0:T(8,128)(2,1)} custom-call(bf16[32,32,16,128]{3,2,1,0:T(8,128)(2,1)S(1)} %copy-done.4, bf16[32,16,8,64]{3,2,1,0:T(8,128)(2,1)S(1)} %copy-done.3, bf16[32,64,128]{2,1,0:T(8,128)(2,1)S(1)} %bitcast.196, bf16[64,64]{1,0:T(8,128)(2,1)S(1)} %bitcast.198, bf16[256,256]{1,0:T(8,128)(2,1)S(1)} %fusion.34.mixing, ...), custom_call_target="tpu_custom_call" | custom-call | tf_op jit(solution)/shard_map/merge_call/pallas_call | solution.py:359
  (111 shorter events, 43.8 us)
Async XLA Ops:
  0.0 142.0 %copy-start = (bf16[32,32]{1,0:T(8,128)(2,1)S(1)}, bf16[32,32]{1,0:T(8,128)(2,1)}, u32[]{:S(2)}) copy-start(bf16[32,32]{1,0:T(8,128)(2,1)} %param.9) | copy-start | bytes 6148
  12.7 30.1 %all-to-all-start = ((bf16[4,8,64,512]{3,2,1,0:T(8,128)(2,1)}), bf16[4,8,64,512]{3,2,1,0:T(8,128)(2,1)S(1)}, u32[]{:S(2)}, u32[]{:S(2)}) async-start(bf16[4,8,64,512]{3,2,1,0:T(8,128)(2,1)} %bitcast.200), calls=%async_computation | async-start | bytes 4194304 | tf_op jit(solution)/shard_map/all_to_all | solution.py:45
  42.7 1.3 copy-start.5
  48.5 20.4 %all-to-all-start.1 = ((bf16[8,8,2,4,512]{4,3,2,1,0:T(4,128)(2,1)}), bf16[8,8,2,4,512]{4,3,2,1,0:T(4,128)(2,1)S(1)}, u32[]{:S(2)}, u32[]{:S(2)}) async-start(bf16[8,8,2,4,512]{4,3,2,1,0:T(4,128)(2,1)} %rows_call.2), calls=%async_computation.1 | async-start | bytes 1048576 | tf_op jit(solution)/shard_map/all_to_all | solution.py:45
  71.9 8.3 %all-to-all-start.2 = ((bf16[4,2,8192]{2,1,0:T(2,128)(2,1)}), bf16[4,2,8192]{2,1,0:T(2,128)(2,1)S(1)}, u32[]{:S(2)}, u32[]{:S(2)}) async-start(bf16[4,2,8192]{2,1,0:T(2,128)(2,1)} %reshape.1102), calls=%async_computation.2 | async-start | bytes 262144 | tf_op jit(solution)/shard_map/all_to_all | solution.py:45
  101.4 8.3 %all-to-all-start.3 = ((bf16[4,2,8192]{2,1,0:T(2,128)(2,1)}), bf16[4,2,8192]{2,1,0:T(2,128)(2,1)S(1)}, u32[]{:S(2)}, u32[]{:S(2)}) async-start(bf16[4,2,8192]{2,1,0:T(2,128)(2,1)} %reshape.1104), calls=%async_computation.3 | async-start | bytes 262144 | tf_op jit(solution)/shard_map/all_to_all | solution.py:45
  110.8 6.3 %copy-start.9 = (f32[32]{0:T(128)S(1)}, f32[32]{0:T(128)}, u32[]{:S(2)}) copy-start(f32[32]{0:T(128)} %param.10) | copy-start | bytes 388
  113.4 18.8 %all-to-all-start.4 = ((bf16[8,8,2,4,512]{4,3,2,1,0:T(4,128)(2,1)}), bf16[8,8,2,4,512]{4,3,2,1,0:T(4,128)(2,1)S(1)}, u32[]{:S(2)}, u32[]{:S(2)}) async-start(bf16[8,8,2,4,512]{4,3,2,1,0:T(4,128)(2,1)} %copy.70), calls=%async_computation.4 | async-start | bytes 1048576 | tf_op jit(solution)/shard_map/all_to_all | solution.py:45
  132.1 0.8 copy-start.7
  137.4 28.4 %all-to-all-start.5 = ((bf16[4,8,64,512]{3,2,1,0:T(8,128)(2,1)}), bf16[4,8,64,512]{3,2,1,0:T(8,128)(2,1)S(1)}, u32[]{:S(2)}, u32[]{:S(2)}) async-start(bf16[4,8,64,512]{3,2,1,0:T(8,128)(2,1)} %rows_back_call.2), calls=%async_computation.5 | async-start | bytes 4194304 | tf_op jit(solution)/shard_map/all_to_all | solution.py:45
  183.0 1.0 copy-start.2
  193.8 11.0 %all-to-all-start.6 = ((bf16[4,8,64,128]{3,2,1,0:T(8,128)(2,1)}), bf16[4,8,64,128]{3,2,1,0:T(8,128)(2,1)S(1)}, u32[]{:S(2)}, u32[]{:S(2)}) async-start(bf16[4,8,64,128]{3,2,1,0:T(8,128)(2,1)} %bitcast.205), calls=%async_computation.6 | async-start | bytes 1048576 | tf_op jit(solution)/shard_map/all_to_all | solution.py:45
  204.8 0.8 copy-start.6
  209.7 13.1 %all-to-all-start.7 = ((bf16[8,8,2,4,256]{4,3,2,1,0:T(4,128)(2,1)}), bf16[8,8,2,4,256]{4,3,2,1,0:T(4,128)(2,1)S(1)}, u32[]{:S(2)}, u32[]{:S(2)}) async-start(bf16[8,8,2,4,256]{4,3,2,1,0:T(4,128)(2,1)} %rows_call.3), calls=%async_computation.7 | async-start | bytes 524288 | tf_op jit(solution)/shard_map/all_to_all | solution.py:45
  225.1 9.5 %all-to-all-start.8 = ((bf16[4,2,8192]{2,1,0:T(2,128)(2,1)}), bf16[4,2,8192]{2,1,0:T(2,128)(2,1)S(1)}, u32[]{:S(2)}, u32[]{:S(2)}) async-start(bf16[4,2,8192]{2,1,0:T(2,128)(2,1)} %reshape.1106), calls=%async_computation.8 | async-start | bytes 262144 | tf_op jit(solution)/shard_map/all_to_all | solution.py:45
  255.8 8.9 %all-to-all-start.9 = ((bf16[4,2,8192]{2,1,0:T(2,128)(2,1)}), bf16[4,2,8192]{2,1,0:T(2,128)(2,1)S(1)}, u32[]{:S(2)}, u32[]{:S(2)}) async-start(bf16[4,2,8192]{2,1,0:T(2,128)(2,1)} %reshape.1108), calls=%async_computation.9 | async-start | bytes 262144 | tf_op jit(solution)/shard_map/all_to_all | solution.py:45
  266.1 22.3 %copy-start.10 = (f32[32]{0:T(128)S(1)}, f32[32]{0:T(128)}, u32[]{:S(2)}) copy-start(f32[32]{0:T(128)} %param.13) | copy-start | bytes 388
  266.1 22.4 %copy-start.11 = (bf16[32,32]{1,0:T(8,128)(2,1)S(1)}, bf16[32,32]{1,0:T(8,128)(2,1)}, u32[]{:S(2)}) copy-start(bf16[32,32]{1,0:T(8,128)(2,1)} %param.12) | copy-start | bytes 6148
  267.0 29.3 %copy-start.3 = (bf16[32,16,8,64]{3,2,1,0:T(8,128)(2,1)S(1)}, bf16[32,16,8,64]{3,2,1,0:T(8,128)(2,1)}, u32[]{:S(2)}) copy-start(bf16[32,16,8,64]{3,2,1,0:T(8,128)(2,1)} %copy-done.2) | copy-start | bytes 1572868
  267.0 13.2 %all-to-all-start.10 = ((bf16[8,8,2,4,256]{4,3,2,1,0:T(4,128)(2,1)}), bf16[8,8,2,4,256]{4,3,2,1,0:T(4,128)(2,1)S(1)}, u32[]{:S(2)}, u32[]{:S(2)}) async-start(bf16[8,8,2,4,256]{4,3,2,1,0:T(4,128)(2,1)} %copy.79), calls=%async_computation.10 | async-start | bytes 524288 | tf_op jit(solution)/shard_map/all_to_all | solution.py:45
  280.2 0.7 copy-start.8
  284.9 11.4 %all-to-all-start.11 = ((bf16[4,8,64,128]{3,2,1,0:T(8,128)(2,1)}), bf16[4,8,64,128]{3,2,1,0:T(8,128)(2,1)S(1)}, u32[]{:S(2)}, u32[]{:S(2)}) async-start(bf16[4,8,64,128]{3,2,1,0:T(8,128)(2,1)} %rows_back_call.3), calls=%async_computation.11 | async-start | bytes 1048576 | tf_op jit(solution)/shard_map/all_to_all | solution.py:45
  296.3 2.2 copy-start.4
  298.5 6.9 %copy-start.1 = (bf16[32,32]{1,0:T(8,128)(2,1)S(1)}, bf16[32,32]{1,0:T(8,128)(2,1)}, u32[]{:S(2)}) copy-start(bf16[32,32]{1,0:T(8,128)(2,1)} %param.9) | copy-start | bytes 6148
